TPU v7x, 512 devices: a whole 4x8x8 slice. The times are simulated.
512 devices in a mesh: seq: 64 (over y, x, core), head: 8 (over z).
Axes of the slice: x: 4, y: 8, z: 8, core: 2. Of those that a mesh axis runs over, the one named last changes fastest.
Arguments:
- queries: bfloat16 [8192, 4096], P('seq', 'head'), may hold values from -0.71875 to 0.71875
- key_rows: bfloat16 [8192, 4096], P('seq', 'head'), may hold values from -0.71875 to 0.71875
- value_rows: bfloat16 [8192, 4096], P('seq', 'head'), may hold values from -0.71875 to 0.71875
- segment_ids: int32 [8192], P('seq'), may hold values from 0 to 7, never falling along the last dimension, each value on 1 to 2048 neighbouring positions
- decay_span: float32 [32], P('head'), may hold values from 30 to 81920, as said below
- norm_gain: float32 [4096], P('head'), may hold values from 0.5 to 1.5
- out_grad: bfloat16 [8192, 4096], P('seq', 'head'), may hold values from -0.71875 to 0.71875
Outputs:
- query_grad: bfloat16 [8192, 4096], P('seq', 'head')
- key_grad: bfloat16 [8192, 4096], P('seq', 'head')
- value_grad: bfloat16 [8192, 4096], P('seq', 'head')
- gain_grad: float32 [4096], P('head')
Inputs may be any that keep to these rules, and one draw needn't show every extreme that they name: segment_ids never falls along the segment; every document of the 8 has a token and the longest has 2048. The decay per token of head h is exp(-1 / decay_span[h]).
All inputs are finite; a program needn't handle non-finite values.
Results may differ from a plain program's by a relative error of at most 0.0012.
Values sent between devices are 32-bit elements; how exact they have to be, the bound alone decides.
A program may use at most 64 MiB of HBM per device.

v0:
```python
import jax
import jax.numpy as jnp
from jax import lax
from jax.sharding import PartitionSpec as P

HEADS = 32
HEAD_DIM = 128
exact = lax.Precision.HIGHEST


def prefix_2(part, axis, combine, identity, reverse):
    count = lax.axis_size(axis)
    place = lax.axis_index(axis)
    ahead = count - 1 - place if reverse else place
    gathered = jax.tree.map(lambda a: lax.all_gather(a, axis), part)
    state = jax.tree.map(lambda a, e: jnp.zeros_like(a) + jnp.asarray(e, a.dtype), part, identity)

    def one(step, state):
        source = count - 1 - step if reverse else step
        return combine(
            state, jax.tree.map(lambda a: lax.dynamic_index_in_dim(a, source, 0, False), gathered)
        )

    return lax.fori_loop(0, ahead, one, state)


def combine_forward(earlier, later):
    state_early, decay_early, first_early, last_early = earlier
    state_late, decay_late, first_late, last_late = later
    passes = jnp.logical_or(
        jnp.logical_and(first_late == last_late, first_late == last_early), first_late < 0
    )
    factor = jnp.where(passes, decay_late, 0.0)
    return (
        state_late + factor[:, None, None] * state_early,
        decay_early * decay_late,
        jnp.where(first_early < 0, first_late, first_early),
        jnp.where(last_late < 0, last_early, last_late),
    )


def combine_backward(earlier, later):
    state_high, decay_high, first_high, last_high = earlier
    state_low, decay_low, first_low, last_low = later
    passes = jnp.logical_or(
        jnp.logical_and(first_low == last_low, last_low == first_high), first_low < 0
    )
    factor = jnp.where(passes, decay_low, 0.0)
    return (
        state_low + factor[:, None, None] * state_high,
        decay_high * decay_low,
        jnp.where(first_low < 0, first_high, first_low),
        jnp.where(last_high < 0, last_low, last_high),
    )


def local(queries, key_rows, value_rows, segment_ids, decay_span, norm_gain, out_grad):
    tok_rows = queries.shape[0]
    heads_here = decay_span.shape[0]
    all_features = HEADS * HEAD_DIM
    block_rows = min(tok_rows, 512)
    block_count = tok_rows // block_rows
    seg_float = segment_ids.astype(jnp.float32)
    positions = jnp.arange(tok_rows, dtype=jnp.float32)
    first_seg = seg_float[0]
    last_seg = seg_float[-1]
    query_full = queries.reshape(tok_rows, heads_here, HEAD_DIM).astype(jnp.float32)
    key_full = key_rows.reshape(tok_rows, heads_here, HEAD_DIM).astype(jnp.float32)
    value_full = value_rows.reshape(tok_rows, heads_here, HEAD_DIM).astype(jnp.float32)
    shard_decay = jnp.exp(-tok_rows / decay_span)
    tail_on = jnp.where(
        (seg_float == last_seg)[:, None],
        jnp.exp(-(tok_rows - 1.0 - positions)[:, None] / decay_span[None, :]),
        0.0,
    )
    local_state = jnp.einsum(
        "thi,thj->hij", key_full * tail_on[:, :, None], value_full, precision=exact
    )
    summary = (local_state, shard_decay, first_seg, last_seg)
    identity = (
        jnp.zeros_like(local_state),
        jnp.ones_like(decay_span),
        jnp.float32(-1.0),
        jnp.float32(-1.0),
    )
    prefix = prefix_2(summary, "seq", combine_forward, identity, False)
    state_in = prefix[0]
    prev_seg = prefix[3]
    offsets = jnp.arange(block_rows, dtype=jnp.float32)
    offset_gap = offsets[:, None] - offsets[None, :]
    causal = offset_gap >= 0
    decay_tile = jnp.where(
        causal[None], jnp.exp(-jnp.maximum(offset_gap, 0.0)[None] / decay_span[:, None, None]), 0.0
    )
    into_weight = jnp.exp(-(offsets + 1.0)[:, None] / decay_span[None, :])
    tail_weight = jnp.exp(-(block_rows - 1.0 - offsets)[:, None] / decay_span[None, :])
    start_weight = jnp.exp(-offsets[:, None] / decay_span[None, :])
    next_weight = jnp.exp(-(block_rows - offsets)[:, None] / decay_span[None, :])
    whole_weight = jnp.exp(-block_rows / decay_span)
    query_blocks = query_full.reshape(block_count, block_rows, heads_here, HEAD_DIM)
    key_blocks = key_full.reshape(block_count, block_rows, heads_here, HEAD_DIM)
    value_blocks = value_full.reshape(block_count, block_rows, heads_here, HEAD_DIM)
    grad_blocks = out_grad.reshape(block_count, block_rows, heads_here * HEAD_DIM)
    seg_blocks = seg_float.reshape(block_count, block_rows)

    def forward_step(carry, inputs):
        state_now, carry_seg, gain_acc = carry
        query_blk, key_blk, value_blk, dy_blk, seg_blk = inputs
        dy_full = dy_blk.astype(jnp.float32)
        same_doc = (seg_blk[:, None] == seg_blk[None, :]).astype(jnp.float32)
        weights = decay_tile * same_doc[None]
        scores = jnp.einsum("thd,shd->hts", query_blk, key_blk, precision=exact) * weights
        inter_on = jnp.where((seg_blk == carry_seg)[:, None], into_weight, 0.0)
        attended = jnp.einsum("hts,shd->thd", scores, value_blk, precision=exact)
        attended = attended + inter_on[:, :, None] * jnp.einsum(
            "thi,hij->thj", query_blk, state_now, precision=exact
        )
        flat_out = attended.reshape(block_rows, heads_here * HEAD_DIM)
        square_part = jnp.sum(flat_out * flat_out, axis=1)
        cross_part = jnp.sum(dy_full * norm_gain[None, :] * flat_out, axis=1)
        square_total, cross_total = lax.psum((square_part, cross_part), "head")
        inv_scale = lax.rsqrt(square_total / all_features + 1e-06)
        out_back = (
            norm_gain[None, :] * dy_full * inv_scale[:, None]
            - flat_out * (inv_scale * inv_scale * inv_scale * cross_total / all_features)[:, None]
        )
        gain_acc = gain_acc + jnp.sum(dy_full * flat_out * inv_scale[:, None], axis=0)
        back_heads = out_back.reshape(block_rows, heads_here, HEAD_DIM)
        grad_scores = jnp.einsum("thd,shd->hts", back_heads, value_blk, precision=exact) * weights
        query_part = jnp.einsum("hts,shd->thd", grad_scores, key_blk, precision=exact)
        query_part = query_part + inter_on[:, :, None] * jnp.einsum(
            "thj,hij->thi", back_heads, state_now, precision=exact
        )
        tail_blk = jnp.where((seg_blk == seg_blk[-1])[:, None], tail_weight, 0.0)
        passes = jnp.logical_and(seg_blk[0] == seg_blk[-1], seg_blk[0] == carry_seg)
        factor = jnp.where(passes, whole_weight, 0.0)
        new_state = (
            jnp.einsum("thi,thj->hij", key_blk * tail_blk[:, :, None], value_blk, precision=exact)
            + factor[:, None, None] * state_now
        )
        outputs = (
            back_heads,
            query_part.reshape(block_rows, heads_here * HEAD_DIM).astype(jnp.bfloat16),
        )
        return ((new_state, seg_blk[-1], gain_acc), outputs)

    start_carry = (state_in, prev_seg, jnp.zeros((heads_here * HEAD_DIM,), jnp.float32))
    forward_carry, forward_out = lax.scan(
        forward_step, start_carry, (query_blocks, key_blocks, value_blocks, grad_blocks, seg_blocks)
    )
    back_blocks = forward_out[0]
    query_grad = forward_out[1].reshape(tok_rows, heads_here * HEAD_DIM)
    gain_local = forward_carry[2]
    back_all = back_blocks.reshape(tok_rows, heads_here, HEAD_DIM)
    start_on = jnp.where(
        (seg_float == first_seg)[:, None], jnp.exp(-positions[:, None] / decay_span[None, :]), 0.0
    )
    local_grad = jnp.einsum(
        "thi,thj->hij", query_full * start_on[:, :, None], back_all, precision=exact
    )
    back_summary = (local_grad, shard_decay, first_seg, last_seg)
    suffix = prefix_2(back_summary, "seq", combine_backward, identity, True)
    grad_in = suffix[0]
    next_seg = suffix[2]

    def backward_step(carry, inputs):
        grad_state, carry_seg = carry
        query_blk, key_blk, value_blk, back_heads, seg_blk = inputs[:5]
        same_doc = (seg_blk[:, None] == seg_blk[None, :]).astype(jnp.float32)
        weights = decay_tile * same_doc[None]
        scores = jnp.einsum("thd,shd->hts", query_blk, key_blk, precision=exact) * weights
        grad_scores = jnp.einsum("thd,shd->hts", back_heads, value_blk, precision=exact) * weights
        key_part = jnp.einsum("hts,thd->shd", grad_scores, query_blk, precision=exact)
        value_part = jnp.einsum("hts,thd->shd", scores, back_heads, precision=exact)
        back_on = jnp.where((seg_blk == carry_seg)[:, None], next_weight, 0.0)
        key_part = key_part + back_on[:, :, None] * jnp.einsum(
            "hij,shj->shi", grad_state, value_blk, precision=exact
        )
        value_part = value_part + back_on[:, :, None] * jnp.einsum(
            "hij,shi->shj", grad_state, key_blk, precision=exact
        )
        start_blk = jnp.where((seg_blk == seg_blk[0])[:, None], start_weight, 0.0)
        passes = jnp.logical_and(seg_blk[0] == seg_blk[-1], seg_blk[-1] == carry_seg)
        factor = jnp.where(passes, whole_weight, 0.0)
        new_state = (
            jnp.einsum(
                "thi,thj->hij", query_blk * start_blk[:, :, None], back_heads, precision=exact
            )
            + factor[:, None, None] * grad_state
        )
        return (
            (new_state, seg_blk[0]),
            (
                key_part.reshape(block_rows, heads_here * HEAD_DIM).astype(jnp.bfloat16),
                value_part.reshape(block_rows, heads_here * HEAD_DIM).astype(jnp.bfloat16),
            ),
        )

    backward_inputs = (query_blocks, key_blocks, value_blocks, back_blocks, seg_blocks)
    _, (key_grad, value_grad) = lax.scan(
        backward_step, (grad_in, next_seg), backward_inputs, reverse=True
    )
    gain_grad = lax.psum(gain_local, "seq")
    return (
        query_grad,
        key_grad.reshape(tok_rows, heads_here * HEAD_DIM),
        value_grad.reshape(tok_rows, heads_here * HEAD_DIM),
        gain_grad,
    )


def solution(mesh):
    in_specs = (
        P("seq", "head"),
        P("seq", "head"),
        P("seq", "head"),
        P("seq"),
        P("head"),
        P("head"),
        P("seq", "head"),
    )
    out_specs = (P("seq", "head"), P("seq", "head"), P("seq", "head"), P("head"))
    return jax.shard_map(local, mesh=mesh, in_specs=in_specs, out_specs=out_specs, check_vma=False)
```

profile of v0, /device:TPU:64, one launch (start us, length us, event | category | flops | bytes accessed | tf_op | source)
XLA Modules:
  0.0 1051.4 jit_solution(12014305828025439504)
XLA Ops:
  9.0 1.3 dynamic-slice.3
  10.3 1.2 fusion.42
  11.5 2.0 broadcast_compare_fusion.1
  18.4 131.0 %all-reduce.3 = (f32[64]{0:T(128)S(1)}, f32[64]{0:T(128)S(1)}, f32[256]{0:T(256)S(1)}) all-reduce(f32[64]{0:T(128)S(1)} %slice_dynamic-update-slice_fusion, f32[64]{0:T(128)S(1)} %get-tuple-element.353, f32[256]{0:T(256)S(1)} %exponential_dynamic-update-slice_fusion), channel_id=1, replica_groups=mesh['seq'=64,'head'=8] {'seq'}, use_global_device_ids=true, to_apply=%add | all-reduce | flops 384 | bytes 3072
  150.7 1.1 convolution_multiply_fusion.1
  154.1 20.0 %psum.23 = f32[128]{0:T(128)S(1)} all-reduce(f32[128]{0:T(128)S(1)} %get-tuple-element.355), channel_id=1, replica_groups=mesh['seq'=64,'head'=8] {'head'}, use_global_device_ids=true, to_apply=%region_3.4 | all-reduce | flops 128 | bytes 1024 | tf_op jit(solution)/shard_map/while/body/eval_jaxpr/psum | solution.py:121
  175.0 16.9 %psum.24 = f32[128]{0:T(128)S(1)} all-reduce(f32[128]{0:T(128)S(1)} %get-tuple-element.312), channel_id=1, replica_groups=mesh['seq'=64,'head'=8] {'head'}, use_global_device_ids=true, to_apply=%region_5.6 | all-reduce | flops 128 | bytes 1024 | tf_op jit(solution)/shard_map/while/body/eval_jaxpr/psum | solution.py:121
  192.7 1.4 fusion.15
  196.8 503.1 %psum.25 = f32[512]{0:T(512)} all-reduce(f32[512]{0:T(512)S(1)} %bitcast.146), channel_id=1, replica_groups=mesh['seq'=64,'head'=8] {'seq'}, use_global_device_ids=true, to_apply=%region_9.10 | all-reduce | flops 512 | bytes 4096 | tf_op jit(solution)/shard_map/psum | solution.py:203
  700.6 341.5 %while.9 = (s32[]{:T(128)}, f32[4,128,128]{2,1,0:T(8,128)S(1)}, f32[]{:T(128)}, s32[]{:T(128)}, f32[64,4,128,128]{3,2,1,0:T(8,128)}, /*index=5*/f32[64]{0:T(128)...) while((s32[]{:T(128)}, f32[4,128,128]{2,1,0:T(8,128)S(1)}, ...), condition=%wide.region_7.8_spmd, body=%wide.region_6.7_spmd.sunk | while | flops 131088 | bytes 786738 | solution.py:24
  709.8 1.1 bitcast_add_fusion.5
  715.3 1.1 bitcast_add_fusion.5
  726.1 1.1 bitcast_add_fusion.5
  731.5 1.1 bitcast_add_fusion.5
  742.4 1.1 bitcast_add_fusion.5
  747.8 1.1 bitcast_add_fusion.5
  758.6 1.1 bitcast_add_fusion.5
  764.1 1.1 bitcast_add_fusion.5
  780.3 1.1 bitcast_add_fusion.5
  785.7 1.1 bitcast_add_fusion.5
  796.6 1.1 bitcast_add_fusion.5
  802.0 1.1 bitcast_add_fusion.5
  812.8 1.1 bitcast_add_fusion.5
  818.3 1.1 bitcast_add_fusion.5
  829.1 1.1 bitcast_add_fusion.5
  834.5 1.1 bitcast_add_fusion.5
  845.4 1.1 bitcast_add_fusion.5
  850.8 1.1 bitcast_add_fusion.5
  861.6 1.1 bitcast_add_fusion.5
  867.0 1.1 bitcast_add_fusion.5
  883.3 1.1 bitcast_add_fusion.5
  888.7 1.1 bitcast_add_fusion.5
  (285 shorter events, 139.6 us)
Async XLA Ops:
  7.2 7.1 copy-start
  7.2 1035.0 %copy-start.3 = (s32[128]{0:T(128)S(1)}, s32[128]{0:T(128)}, u32[]{:S(2)}) copy-start(s32[128]{0:T(128)} %param.14) | copy-start | bytes 1540
  7.2 1036.2 %copy-start.1 = (bf16[128,512]{1,0:T(8,128)(2,1)S(1)}, bf16[128,512]{1,0:T(8,128)(2,1)}, u32[]{:S(2)}) copy-start(bf16[128,512]{1,0:T(8,128)(2,1)} %param.12) | copy-start | bytes 393220
  7.2 1035.0 %copy-start.2 = (f32[4]{0:T(128)S(1)}, f32[4]{0:T(128)}, u32[]{:S(2)}) copy-start(f32[4]{0:T(128)} %param.15) | copy-start | bytes 52
  7.2 145.1 %all-gather.6.cloned.1.call-start = ((), (), s32[]{:S(2)}) async-start(), calls=%async_computation | async-start | bytes 17039360 | tf_op jit(solution)/shard_map/all_gather | solution.py:15
  15.2 685.4 %all-gather.8.cloned.1.call-start = ((), (), s32[]{:S(2)}) async-start(), calls=%async_computation.1 | async-start | bytes 17039360 | tf_op jit(solution)/shard_map/all_gather | solution.py:15
Sparse Core Ops, SparseCore 0:
  15.3 108.7 all-gather.5
  194.2 470.6 all-gather.7
where the time goes:
time: 1060 us; the launch traced here: 1050 us
  blocking collectives  671 us (63%)
  loops' own time  196 us (18%)
  local copies, waits for them, and re-layouts  87 us (8%)
  other arithmetic  75.2 us (7%)
  between operations  14.9 us (1%)
    psum x1, blocking collectives, local(): gain_grad = lax.psum(gain_local, 'seq')  503 us
    another operation x2, loops' own time, prefix_2(): return lax.fori_loop(0, ahead, one, state)  196 us
    unnamed x1, blocking collectives  131 us
    dynamic_slice x126, local copies, waits for them, and re-layouts, one(): lax.dynamic_index_in_dim(a, source, 0, False)  78.2 us
    add x63, other arithmetic, combine_backward(): state_low + factor[:, None, None] * state_high  66.8 us
    psum x2, blocking collectives, forward_step(): square_total, cross_total = lax.psum((square_part, cross_part), 'head')  36.8 us
  transfers between devices with their start and end apart: 2, of which 0 were waited for; matrix products, arithmetic and copies ran while one was open for 1% of the time, Pallas kernels for 0%

commit v1 on v0

--- a/solution.py
+++ b/solution.py
@@ -200,7 +200,8 @@
     _, (key_grad, value_grad) = lax.scan(
         backward_step, (grad_in, next_seg), backward_inputs, reverse=True
     )
-    gain_grad = lax.psum(gain_local, "seq")
+    blocks = lax.all_gather(gain_local, "seq", axis=0, tiled=False)
+    gain_grad = blocks.sum(axis=0)
     return (
         query_grad,
         key_grad.reshape(tok_rows, heads_here * HEAD_DIM),

time: 1060 us -> 1020 us (0.962)
  blocking collectives: 671 us -> 589 us
  waiting for transfers between devices: 0.07 us -> 45.6 us
    psum x1 -> x0, blocking collectives: 503 us -> none  [local(): gain_grad = lax.psum(gain_local, 'seq')]
    all_gather x0 -> x1, blocking collectives: none -> 421 us  [local(): blocks = lax.all_gather(gain_local, 'seq', axis=0, tiled=False)]
    all_gather x2, waiting for transfers between devices: 0.04 us -> 45.5 us  [prefix_2(): gathered = jax.tree.map(lambda a: lax.all_gather(a, axis), part)]
  transfers between devices with their start and end apart: 2 -> 2, of which waited for: 0 -> 1; matrix products, arithmetic and copies ran while one was open for 1% -> 1% of each run, Pallas kernels for 0% -> 0%
where the time goes in v1:
time: 1020 us
  blocking collectives  589 us (58%)
  loops' own time  196 us (19%)
  local copies, waits for them, and re-layouts  87.1 us (9%)
  other arithmetic  75.9 us (7%)
  waiting for transfers between devices  45.6 us (4%)
  between operations  14.9 us (1%)
    all_gather x1, blocking collectives, local(): blocks = lax.all_gather(gain_local, 'seq', axis=0, tiled=False)  421 us
    another operation x2, loops' own time, prefix_2(): return lax.fori_loop(0, ahead, one, state)  196 us
    unnamed x1, blocking collectives  131 us
    dynamic_slice x126, local copies, waits for them, and re-layouts, one(): lax.dynamic_index_in_dim(a, source, 0, False)  78.4 us
    add x63, other arithmetic, combine_backward(): state_low + factor[:, None, None] * state_high  66.8 us
    all_gather x2, waiting for transfers between devices, prefix_2(): gathered = jax.tree.map(lambda a: lax.all_gather(a, axis), part)  45.5 us
    psum x2, blocking collectives, forward_step(): square_total, cross_total = lax.psum((square_part, cross_part), 'head')  36.8 us
  transfers between devices with their start and end apart: 2, of which 1 were waited for; matrix products, arithmetic and copies ran while one was open for 1% of the time, Pallas kernels for 0%

profile of v1, /device:TPU:64, one launch (start us, length us, event | category | flops | bytes accessed | tf_op | source)
XLA Modules:
  0.0 1015.6 jit_solution(15957905365908901342)
XLA Ops:
  9.0 1.3 dynamic-slice.3
  10.3 1.2 fusion.42
  11.5 2.0 broadcast_compare_fusion.1
  18.4 131.0 %all-reduce.3 = (f32[64]{0:T(128)S(1)}, f32[64]{0:T(128)S(1)}, f32[256]{0:T(256)S(1)}) all-reduce(f32[64]{0:T(128)S(1)} %slice_dynamic-update-slice_fusion, f32[64]{0:T(128)S(1)} %get-tuple-element.353, f32[256]{0:T(256)S(1)} %exponential_dynamic-update-slice_fusion), channel_id=1, replica_groups=mesh['seq'=64,'head'=8] {'seq'}, use_global_device_ids=true, to_apply=%add | all-reduce | flops 384 | bytes 3072
  150.7 1.1 convolution_multiply_fusion.1
  154.1 20.0 %psum.16 = f32[128]{0:T(128)S(1)} all-reduce(f32[128]{0:T(128)S(1)} %get-tuple-element.355), channel_id=1, replica_groups=mesh['seq'=64,'head'=8] {'head'}, use_global_device_ids=true, to_apply=%region_3.4 | all-reduce | flops 128 | bytes 1024 | tf_op jit(solution)/shard_map/while/body/eval_jaxpr/psum | solution.py:121
  175.0 16.9 %psum.17 = f32[128]{0:T(128)S(1)} all-reduce(f32[128]{0:T(128)S(1)} %get-tuple-element.312), channel_id=1, replica_groups=mesh['seq'=64,'head'=8] {'head'}, use_global_device_ids=true, to_apply=%region_5.6 | all-reduce | flops 128 | bytes 1024 | tf_op jit(solution)/shard_map/while/body/eval_jaxpr/psum | solution.py:121
  192.7 1.4 fusion.15
  196.8 420.9 %all-gather.3 = f32[64,1,512]{2,1,0:T(1,128)S(1)} all-gather(f32[1,1,512]{2,1,0:T(1,128)S(1)} %bitcast.146), channel_id=1, replica_groups=mesh['seq'=64,'head'=8] {'seq'}, dimensions={0}, use_global_device_ids=true | all-gather | bytes 133120 | tf_op jit(solution)/shard_map/all_gather | solution.py:203
  619.1 45.5 %all-gather.9.cloned.1.call-done = f32[256,128,128]{2,1,0:T(8,128)} async-done(((f32[4,128,128]{2,1,0:T(8,128)}), f32[256,128,128]{2,1,0:T(8,128)}) %all-gather.9.cloned.1.call-update) | async-done | bytes 16777232 | tf_op jit(solution)/shard_map/all_gather | solution.py:15
  664.6 341.6 %while.9 = (s32[]{:T(128)}, f32[4,128,128]{2,1,0:T(8,128)S(1)}, f32[]{:T(128)}, s32[]{:T(128)}, f32[64,4,128,128]{3,2,1,0:T(8,128)}, /*index=5*/f32[64]{0:T(128)...) while((s32[]{:T(128)}, f32[4,128,128]{2,1,0:T(8,128)S(1)}, ...), condition=%wide.region_7.8_spmd, body=%wide.region_6.7_spmd.sunk | while | flops 131088 | bytes 786738 | solution.py:24
  668.4 1.1 bitcast_add_fusion.5
  679.3 1.1 bitcast_add_fusion.5
  684.7 1.1 bitcast_add_fusion.5
  695.5 1.1 bitcast_add_fusion.5
  706.4 1.1 bitcast_add_fusion.5
  717.2 1.1 bitcast_add_fusion.5
  722.6 1.1 bitcast_add_fusion.5
  733.5 1.1 bitcast_add_fusion.5
  744.3 1.1 bitcast_add_fusion.5
  749.8 1.1 bitcast_add_fusion.5
  755.2 1.1 bitcast_add_fusion.5
  760.6 1.1 bitcast_add_fusion.5
  771.5 1.1 bitcast_add_fusion.5
  782.3 1.1 bitcast_add_fusion.5
  787.7 1.1 bitcast_add_fusion.5
  798.6 1.1 bitcast_add_fusion.5
  809.4 1.1 bitcast_add_fusion.5
  820.3 1.1 bitcast_add_fusion.5
  825.7 1.1 bitcast_add_fusion.5
  836.5 1.1 bitcast_add_fusion.5
  847.4 1.1 bitcast_add_fusion.5
  (286 shorter events, 141.5 us)
Async XLA Ops:
  7.2 7.1 copy-start
  7.2 999.1 %copy-start.3 = (s32[128]{0:T(128)S(1)}, s32[128]{0:T(128)}, u32[]{:S(2)}) copy-start(s32[128]{0:T(128)} %param.14) | copy-start | bytes 1540
  7.2 1000.4 %copy-start.1 = (bf16[128,512]{1,0:T(8,128)(2,1)S(1)}, bf16[128,512]{1,0:T(8,128)(2,1)}, u32[]{:S(2)}) copy-start(bf16[128,512]{1,0:T(8,128)(2,1)} %param.12) | copy-start | bytes 393220
  7.2 999.1 %copy-start.2 = (f32[4]{0:T(128)S(1)}, f32[4]{0:T(128)}, u32[]{:S(2)}) copy-start(f32[4]{0:T(128)} %param.15) | copy-start | bytes 52
  7.2 145.1 %all-gather.7.cloned.1.call-start = ((), (), s32[]{:S(2)}) async-start(), calls=%async_computation | async-start | bytes 17039360 | tf_op jit(solution)/shard_map/all_gather | solution.py:15
  15.2 649.4 %all-gather.9.cloned.1.call-start = ((), (), s32[]{:S(2)}) async-start(), calls=%async_computation.1 | async-start | bytes 17039360 | tf_op jit(solution)/shard_map/all_gather | solution.py:15
Sparse Core Ops, SparseCore 0:
  15.3 108.7 all-gather.6
  194.2 470.3 all-gather.8
